TPU v7x, 512 devices: a whole 4x4x16 slice. The times are simulated.
512 devices in a mesh: dp: 64 (over z_lo, x, core), mp: 8 (over z_hi, y).
Axes of the slice: x: 4, y: 4, z: 16 (z_hi: 2, z_lo: 8; z = z_hi * 8 + z_lo), core: 2. Of those that a mesh axis runs over, the one named last changes fastest.
Arguments:
- inputs: bfloat16 [1024, 6144], P('dp', 'mp'), may hold values from -6 to 6
- targets: bfloat16 [1024, 6144], P('dp', 'mp'), may hold values from -6 to 6
- w_in: bfloat16 [6144, 16384], P('mp', 'dp'), may hold values from -6 to 6
- w_out: bfloat16 [16384, 6144], P('dp', 'mp'), may hold values from -6 to 6
- teach_in: float32 [6144, 16384], P('mp', 'dp'), may hold values from -6 to 6
- teach_out: float32 [16384, 6144], P('dp', 'mp'), may hold values from -6 to 6
Outputs:
- grad_in: bfloat16 [6144, 16384], P('mp', 'dp')
- grad_out: bfloat16 [16384, 6144], P('dp', 'mp')
- new_in: float32 [6144, 16384], P('mp', 'dp')
- new_out: float32 [16384, 6144], P('dp', 'mp')
All inputs are finite; a program needn't handle non-finite values.
Results may differ from a plain program's by a relative error of at most 0.017.
Values may be sent and summed in bfloat16 or wider, within the bound.
No kernel may reach another device: no remote copies, remote signals or barrier semaphores. Data moves between devices by JAX's collectives and lax.ppermute only.
A program may use at most 64 MiB of HBM per device.

v0:
```python
import math
import jax
import jax.numpy as jnp
from jax import lax
from jax.sharding import Mesh
from jax.sharding import PartitionSpec as P

D = 6144
FF = 16384
DP = ("dp_0", "dp_1", "dp_2")
decay_rate = 0.99
step_size = 0.5


def from_everyone(value, axis):
    copies = jnp.broadcast_to(value, (lax.axis_size(axis), *value.shape))
    return lax.all_to_all(copies, axis, split_axis=0, concat_axis=0, tiled=True)


def in_order(pieces, dim):
    pieces = jnp.moveaxis(pieces, 0, dim)
    dims = pieces.shape
    return pieces.reshape(*dims[:dim], dims[dim] * dims[dim + 1], *dims[dim + 2 :])


def gather_axes(value, axes, dim):
    far, near = axes
    pieces = from_everyone(from_everyone(value, far), near)
    return in_order(pieces.swapaxes(0, 1).reshape(-1, *value.shape), dim)


def cut_along(value, dim, size):
    before, after = (value.shape[:dim], value.shape[dim + 1 :])
    return jnp.moveaxis(value.reshape(*before, size, -1, *after), dim, 0)


def summed_on_arrival(value, axis, dim):
    pieces = cut_along(value, dim, lax.axis_size(axis))
    arrived = lax.all_to_all(pieces, axis, split_axis=0, concat_axis=0, tiled=True)
    return arrived.sum(axis=0)


def sum_in_two_steps(value, axes, dim):
    far, near = axes
    own = summed_on_arrival(cut_along(value, dim, lax.axis_size(far)), near, dim + 1)
    return jnp.sum(lax.all_to_all(own, far, 0, 0, tiled=True), axis=0)


def gelu_value(value):
    return 0.5 * value * (1.0 + jax.scipy.special.erf(value * (1.0 / math.sqrt(2.0))))


def gelu_slope(value):
    normal_cdf = 0.5 * (1.0 + jax.scipy.special.erf(value * (1.0 / math.sqrt(2.0))))
    return normal_cdf + value * jnp.exp(-0.5 * value * value) * (1.0 / math.sqrt(2.0 * math.pi))


def shards(inputs, targets, w_in, w_out, teach_in, teach_out):
    in_scale = 1.0 / math.sqrt(D)
    out_scale = 1.0 / math.sqrt(FF)
    gathered = gather_axes(inputs, (("dp_0", "dp_1"), "dp_2"), 0)
    partial_pre = jnp.dot(gathered, w_in, preferred_element_type=jnp.float32) * in_scale
    preact = lax.psum(partial_pre, "mp")
    hidden = gelu_value(preact).astype(jnp.bfloat16)
    block = hidden
    summed_rows = sum_in_two_steps(
        jnp.dot(block, w_out, preferred_element_type=jnp.float32) * out_scale,
        (("dp_0", "dp_1"), "dp_2"),
        0,
    )
    slope = (inputs.astype(jnp.float32) + summed_rows - targets.astype(jnp.float32)).astype(
        jnp.bfloat16
    )
    piece = gather_axes(slope, (("dp_0", "dp_1"), "dp_2"), 0)
    block = hidden
    grad_acc = jnp.einsum("tf,td->fd", block, piece, preferred_element_type=jnp.float32) * out_scale
    slope_part = (
        jnp.einsum("td,fd->tf", piece, w_out, preferred_element_type=jnp.float32) * out_scale
    )
    hidden_slope = lax.psum(slope_part.astype(jnp.bfloat16), "mp").astype(jnp.float32)
    pre_slope = (hidden_slope * gelu_slope(preact)).astype(jnp.bfloat16)
    grad_in = (
        jnp.einsum("td,tf->df", gathered, pre_slope, preferred_element_type=jnp.float32) * in_scale
    )
    new_in = decay_rate * teach_in + (1.0 - decay_rate) * (
        w_in.astype(jnp.float32) - step_size * grad_in
    )
    new_out = decay_rate * teach_out + (1.0 - decay_rate) * (
        w_out.astype(jnp.float32) - step_size * grad_acc
    )
    return (grad_in.astype(jnp.bfloat16), grad_acc.astype(jnp.bfloat16), new_in, new_out)


def solution(mesh):
    finer = Mesh(mesh.devices.reshape(8, 4, 2, mesh.shape["mp"]), ("dp_0", "dp_1", "dp_2", "mp"))
    return jax.shard_map(
        shards,
        mesh=finer,
        in_specs=(P(DP, "mp"), P(DP, "mp"), P("mp", DP), P(DP, "mp"), P("mp", DP), P(DP, "mp")),
        out_specs=(P("mp", DP), P(DP, "mp"), P("mp", DP), P(DP, "mp")),
        check_vma=False,
    )
```

profile of v0, /device:TPU:2, one launch (start us, length us, event | category | flops | bytes accessed | tf_op | source)
XLA Modules:
  0.0 558.3 jit_solution(2530100006321149228)
XLA Ops:
  7.2 0.8 broadcast_in_dim.12
  8.0 54.8 %all_to_all.30 = bf16[32,16,768]{2,1,0:T(8,128)(2,1)S(1)} all-to-all(bf16[32,16,768]{2,1,0:T(8,128)(2,1)S(1)} %broadcast_in_dim.12), channel_id=1, replica_groups=mesh['dp_0'=8,'dp_1'=4,'dp_2'=2,'mp'=8] {'dp_0','dp_1'}, dimensions={0} | all-to-all | bytes 1572864 | tf_op jit(solution)/shard_map/all_to_all | solution.py:17
  62.8 0.1 broadcast_in_dim.13
  62.9 5.0 all_to_all.31
  67.9 0.2 copy.25
  68.1 0.8 copy-done.1
  68.9 1.6 convolution_multiply_fusion.2
  70.5 0.0 all-reduce.5.cloned.1.call-start
  70.5 172.3 %all-reduce.3.cloned.1.call-done = f32[1024,256]{1,0:T(8,128)} async-done(((f32[1024,256]{1,0:T(8,128)}), f32[1024,256]{1,0:T(8,128)}) %all-reduce.3.cloned.1.call-update) | async-done | bytes 1048592 | tf_op jit(solution)/shard_map/psum | solution.py:63
  242.8 1.4 multiply_convert_fusion
  244.2 0.6 convolution_multiply_fusion
  244.8 0.2 copy-done
  245.0 0.2 copy.33
  245.3 7.2 %all_to_all.32 = f32[2,32,16,768]{3,2,1,0:T(8,128)} all-to-all(f32[2,32,16,768]{3,2,1,0:T(8,128)S(1)} %bitcast.29), channel_id=1, replica_groups=mesh['dp_0'=8,'dp_1'=4,'dp_2'=2,'mp'=8] {'dp_2'}, dimensions={0} | all-to-all | bytes 6291456 | tf_op jit(solution)/shard_map/all_to_all | solution.py:39
  252.5 3.4 reduce_sum.18
  255.9 88.0 %all_to_all.33 = f32[32,16,768]{2,1,0:T(8,128)S(1)} all-to-all(f32[32,16,768]{2,1,0:T(8,128)} %reduce_sum.18), channel_id=1, replica_groups=mesh['dp_0'=8,'dp_1'=4,'dp_2'=2,'mp'=8] {'dp_0','dp_1'}, dimensions={0} | all-to-all | bytes 3145728 | tf_op jit(solution)/shard_map/all_to_all | solution.py:46
  343.9 0.7 reduce_sum.19
  344.6 0.8 subtract_convert_fusion
  345.4 0.1 broadcast_in_dim.14
  345.5 46.4 %all_to_all.34 = bf16[32,16,768]{2,1,0:T(8,128)(2,1)S(1)} all-to-all(bf16[32,16,768]{2,1,0:T(8,128)(2,1)S(1)} %broadcast_in_dim.14), channel_id=1, replica_groups=mesh['dp_0'=8,'dp_1'=4,'dp_2'=2,'mp'=8] {'dp_0','dp_1'}, dimensions={0} | all-to-all | bytes 1572864 | tf_op jit(solution)/shard_map/all_to_all | solution.py:17
  391.9 0.1 broadcast_in_dim.15
  392.0 5.0 all_to_all.35
  397.0 0.2 copy.27
  397.2 1.4 fusion
  398.6 1.2 copy.29
  399.8 2.3 copy.28
  402.1 3.1 multiply_add_fusion
  405.2 141.6 %all-reduce.5.cloned.1.call-done = bf16[1024,256]{1,0:T(8,128)(2,1)} async-done(((bf16[1024,256]{1,0:T(8,128)(2,1)}), bf16[1024,256]{1,0:T(8,128)(2,1)}) %all-reduce.5.cloned.1.call-update) | async-done | bytes 524304 | tf_op jit(solution)/shard_map/psum | solution.py:80
  546.8 2.4 fusion.8
  549.3 0.1 fusion.14
  549.4 0.9 copy.30
  550.3 1.1 copy.31
  (7 shorter events, 0.1 us)
Async XLA Ops:
  7.2 235.6 %all-reduce.3.cloned.1.call-start = ((), (), s32[]{:S(2)}) async-start(), calls=%async_computation.6 | async-start | bytes 2097152 | tf_op jit(solution)/shard_map/psum | solution.py:63
  67.9 1.0 copy-start.1
  70.5 173.8 %copy-start.2 = (bf16[256,768]{1,0:T(8,128)(2,1)S(1)}, bf16[256,768]{1,0:T(8,128)(2,1)}, u32[]{:S(2)}) copy-start(bf16[256,768]{1,0:T(8,128)(2,1)} %param.9) | copy-start | bytes 1179652
  70.5 476.3 %all-reduce.5.cloned.1.call-start = ((), (), s32[]{:S(2)}) async-start(), calls=%async_computation.7 | async-start | bytes 1048576 | tf_op jit(solution)/shard_map/psum | solution.py:80
  244.2 0.8 copy-start
Sparse Core Ops, SparseCore 0:
  70.6 172.1 all-reduce.2
  398.8 148.0 all-reduce.4
where the time goes:
time: 559 us; the launch traced here: 558 us
  waiting for transfers between devices  314 us (56%)
  blocking collectives  206 us (37%)
  between operations  14.1 us (3%)
  matrix products  9.11 us (2%)
  local copies, waits for them, and re-layouts  8.2 us (1%)
  other arithmetic  6.41 us (1%)
    psum x1, waiting for transfers between devices, shards(): preact = lax.psum(partial_pre, 'mp')  172 us
    psum x1, waiting for transfers between devices, shards(): lax.psum(slope_part.astype(jnp.bfloat16), 'mp').astype(jnp.float32)  142 us
    all_to_all x4, blocking collectives, from_everyone(): return lax.all_to_all(copies, axis, split_axis=0, concat_axis=0, tiled=True)  111 us
    all_to_all x1, blocking collectives, sum_in_two_steps(): return jnp.sum(lax.all_to_all(own, far, 0, 0, tiled=True), axis=0)  88 us
  transfers between devices with their start and end apart: 2, of which 2 were waited for; matrix products, arithmetic and copies ran while one was open for 1% of the time, Pallas kernels for 0%

commit v1 on v0

--- a/solution.py
+++ b/solution.py
@@ -60,7 +60,8 @@
     out_scale = 1.0 / math.sqrt(FF)
     gathered = gather_axes(inputs, (("dp_0", "dp_1"), "dp_2"), 0)
     partial_pre = jnp.dot(gathered, w_in, preferred_element_type=jnp.float32) * in_scale
-    preact = lax.psum(partial_pre, "mp")
+    terms = lax.all_gather(partial_pre, "mp")
+    preact = jnp.sum(terms, axis=0)
     hidden = gelu_value(preact).astype(jnp.bfloat16)
     block = hidden
     summed_rows = sum_in_two_steps(

time: 559 us -> 684 us (1.22)
  waiting for transfers between devices: 314 us -> 422 us
  blocking collectives: 206 us -> 217 us
    all_gather x0 -> x1, waiting for transfers between devices: none -> 280 us  [shards(): terms = lax.all_gather(partial_pre, 'mp')]
    psum x1 -> x0, waiting for transfers between devices: 172 us -> none  [shards(): preact = lax.psum(partial_pre, 'mp')]
    all_to_all x1, blocking collectives: 88 us -> 98.8 us  [sum_in_two_steps(): return jnp.sum(lax.all_to_all(own, far, 0, 0, tiled=True), axis=0)]
where the time goes in v1:
time: 684 us; the launch traced here: 683 us
  waiting for transfers between devices  422 us (62%)
  blocking collectives  217 us (32%)
  between operations  14.1 us (2%)
  other arithmetic  10.7 us (2%)
  local copies, waits for them, and re-layouts  9.75 us (1%)
  matrix products  9.12 us (1%)
    all_gather x1, waiting for transfers between devices, shards(): terms = lax.all_gather(partial_pre, 'mp')  280 us
    psum x1, waiting for transfers between devices, shards(): lax.psum(slope_part.astype(jnp.bfloat16), 'mp').astype(jnp.float32)  142 us
    all_to_all x4, blocking collectives, from_everyone(): return lax.all_to_all(copies, axis, split_axis=0, concat_axis=0, tiled=True)  111 us
    all_to_all x1, blocking collectives, sum_in_two_steps(): return jnp.sum(lax.all_to_all(own, far, 0, 0, tiled=True), axis=0)  98.8 us
  transfers between devices with their start and end apart: 2, of which 2 were waited for; matrix products, arithmetic and copies ran while one was open for 1% of the time, Pallas kernels for 0%

profile of v1, /device:TPU:2, one launch (start us, length us, event | category | flops | bytes accessed | tf_op | source)
XLA Modules:
  0.0 683.4 jit_solution(14006469738494107793)
XLA Ops:
  7.2 0.8 broadcast_in_dim.12
  8.0 54.8 %all_to_all.30 = bf16[32,16,768]{2,1,0:T(8,128)(2,1)S(1)} all-to-all(bf16[32,16,768]{2,1,0:T(8,128)(2,1)S(1)} %broadcast_in_dim.12), channel_id=1, replica_groups=mesh['dp_0'=8,'dp_1'=4,'dp_2'=2,'mp'=8] {'dp_0','dp_1'}, dimensions={0} | all-to-all | bytes 1572864 | tf_op jit(solution)/shard_map/all_to_all | solution.py:17
  62.8 0.1 broadcast_in_dim.13
  62.9 5.0 all_to_all.31
  67.9 0.2 copy.25
  68.1 0.8 copy-done.1
  68.9 1.6 convolution_multiply_fusion.2
  70.6 279.9 %all-gather.3.cloned.1.call-done = f32[8192,256]{1,0:T(8,128)} async-done(((f32[1024,256]{1,0:T(8,128)}), f32[8192,256]{1,0:T(8,128)}) %all-gather.3.cloned.1.call-update) | async-done | bytes 8388624 | tf_op jit(solution)/shard_map/all_gather | solution.py:63
  350.5 4.1 reduce_sum.27
  354.5 0.2 multiply_convert_fusion
  354.7 0.8 copy-done.2
  355.5 0.6 convolution_multiply_fusion
  356.1 0.2 copy.33
  356.3 7.2 %all_to_all.32 = f32[2,32,16,768]{3,2,1,0:T(8,128)} all-to-all(f32[2,32,16,768]{3,2,1,0:T(8,128)S(1)} %bitcast.30), channel_id=1, replica_groups=mesh['dp_0'=8,'dp_1'=4,'dp_2'=2,'mp'=8] {'dp_2'}, dimensions={0} | all-to-all | bytes 6291456 | tf_op jit(solution)/shard_map/all_to_all | solution.py:39
  363.6 3.4 reduce_sum.28
  367.0 98.8 %all_to_all.33 = f32[32,16,768]{2,1,0:T(8,128)} all-to-all(f32[32,16,768]{2,1,0:T(8,128)} %reduce_sum.28), channel_id=1, replica_groups=mesh['dp_0'=8,'dp_1'=4,'dp_2'=2,'mp'=8] {'dp_0','dp_1'}, dimensions={0} | all-to-all | bytes 3145728 | tf_op jit(solution)/shard_map/all_to_all | solution.py:46
  465.8 2.1 reduce_sum.29
  467.9 0.8 subtract_convert_fusion
  468.8 46.4 %all_to_all.34 = bf16[32,16,768]{2,1,0:T(8,128)(2,1)S(1)} all-to-all(bf16[32,16,768]{2,1,0:T(8,128)(2,1)S(1)} %broadcast_in_dim.14), channel_id=1, replica_groups=mesh['dp_0'=8,'dp_1'=4,'dp_2'=2,'mp'=8] {'dp_0','dp_1'}, dimensions={0} | all-to-all | bytes 1572864 | tf_op jit(solution)/shard_map/all_to_all | solution.py:17
  515.2 0.1 broadcast_in_dim.15
  515.3 5.0 all_to_all.35
  520.3 0.2 copy.27
  520.6 1.2 copy-done
  521.7 1.4 fusion
  523.1 0.9 copy.29
  524.1 2.3 copy.28
  526.4 3.3 multiply_add_fusion
  529.7 142.5 %all-reduce.2.cloned.1.call-done = bf16[1024,256]{1,0:T(8,128)(2,1)} async-done(((bf16[1024,256]{1,0:T(8,128)(2,1)}), bf16[1024,256]{1,0:T(8,128)(2,1)}) %all-reduce.2.cloned.1.call-update) | async-done | bytes 524304 | tf_op jit(solution)/shard_map/psum | solution.py:81
  672.2 2.2 fusion.8
  674.4 0.1 fusion.14
  674.5 0.9 copy.30
  675.4 1.1 copy.31
  (12 shorter events, 0.2 us)
Async XLA Ops:
  7.2 343.3 %all-gather.3.cloned.1.call-start = ((), (), s32[]{:S(2)}) async-start(), calls=%async_computation.7 | async-start | bytes 9437184 | tf_op jit(solution)/shard_map/all_gather | solution.py:63
  67.9 1.0 copy-start.1
  70.5 601.6 %all-reduce.2.cloned.1.call-start = ((), (), s32[]{:S(2)}) async-start(), calls=%async_computation.6 | async-start | bytes 1048576 | tf_op jit(solution)/shard_map/psum | solution.py:81
  354.5 1.0 copy-start.2
  520.3 1.4 copy-start.3
  520.5 1.2 copy-start
  524.1 2.3 copy-start.4
Sparse Core Ops, SparseCore 0:
  70.7 279.7 all-gather.2
  523.3 148.8 all-reduce.1
